TPU v7x, 128 devices: a whole 4x4x4 slice. The times are simulated.
128 devices in a mesh: section: 2 (over core), dp: 64 (over y, z, x).
Axes of the slice: x: 4, y: 4, z: 4, core: 2. Of those that a mesh axis runs over, the one named last changes fastest.
Arguments:
- inputs: bfloat16 [2, 4096, 960], P(None, 'dp'), may hold values from -16 to 16
- starts: int32 [2, 4096], P(None, 'dp'), may hold values from 0 to 64, as said below
- cotangent: bfloat16 [2, 4096, 960], P(None, 'dp'), may hold values from -16 to 16
- w_query: bfloat16 [2, 960, 960], P('section', 'dp'), may hold values from -0.1875 to 0.1875
- w_key: bfloat16 [2, 960, 320], P('section', 'dp'), may hold values from -0.1875 to 0.1875
- w_value: bfloat16 [2, 960, 320], P('section', 'dp'), may hold values from -0.1875 to 0.1875
- w_output: bfloat16 [2, 960, 960], P('section', 'dp'), may hold values from -0.75 to 0.75
- w_gate: bfloat16 [2, 960, 2560], P('section', 'dp'), may hold values from -0.1875 to 0.1875
- w_up: bfloat16 [2, 960, 2560], P('section', 'dp'), may hold values from -0.1875 to 0.1875
- w_down: bfloat16 [2, 2560, 960], P('section', 'dp'), may hold values from -0.15625 to 0.15625
- attn_gain: bfloat16 [2, 960], P('section', 'dp'), may hold values from 0.25 to 1.75
- ffn_gain: bfloat16 [2, 960], P('section', 'dp'), may hold values from 0.25 to 1.75
Outputs:
- activations: bfloat16 [2, 2, 4096, 960], P('section', None, 'dp')
- input_grads: bfloat16 [2, 2, 4096, 960], P('section', None, 'dp')
- grad_query: float32 [2, 960, 960], P('section', 'dp')
- grad_key: float32 [2, 960, 320], P('section', 'dp')
- grad_value: float32 [2, 960, 320], P('section', 'dp')
- grad_output: float32 [2, 960, 960], P('section', 'dp')
- grad_gate: float32 [2, 960, 2560], P('section', 'dp')
- grad_up: float32 [2, 960, 2560], P('section', 'dp')
- grad_down: float32 [2, 2560, 960], P('section', 'dp')
- grad_attn_gain: float32 [2, 960], P('section', 'dp')
- grad_ffn_gain: float32 [2, 960], P('section', 'dp')
Inputs may be any that keep to these rules, and one draw needn't show every extreme that they name: `starts`: within each aligned block of 64 rows (one index of dp, one micro-batch) sequences lie end to end from the block's first row, each row holding the block-local index of its sequence's first row; the rows after the last sequence are padding and hold 64. At least a quarter of every block's rows are in sequences, and some blocks are full.
All inputs are finite; a program needn't handle non-finite values.
Results may differ from a plain program's by a relative error of at most 0.023.
Values may be sent and summed in bfloat16 or wider, within the bound.
No kernel may reach another device: no remote copies, remote signals or barrier semaphores. Data moves between devices by JAX's collectives and lax.ppermute only.
A program may use at most 256 MiB of HBM per device.

v0:
```python
from functools import partial
import jax
import jax.numpy as jnp
from jax import lax
from jax.sharding import PartitionSpec as P

D = 960
HEADS = 15
KV_HEADS = 5
HEAD_DIM = 64
FF = 2560
QD = 960
KVD = 320
norm_eps = 1e-05
masked_score = -1e30
rope_base = 10000.0


def from_behind(value, axis, steps):
    count = lax.axis_size(axis)
    first, last = (max(0, -steps), min(count, count - steps))
    return lax.ppermute(value, axis, [(source, source + steps) for source in range(first, last)])


def rms_scale(values, gain):
    inverse = lax.rsqrt(jnp.mean(values * values, axis=-1, keepdims=True) + norm_eps)
    return values * inverse * gain


def rotate(values, cosine_table, sine_table):
    half_dim = values.shape[-1] // 2
    first_half = values[..., :half_dim]
    second_half = values[..., half_dim:]
    return jnp.concatenate(
        [
            first_half * cosine_table - second_half * sine_table,
            second_half * cosine_table + first_half * sine_table,
        ],
        axis=-1,
    )


def swiglu(gate_vals, up_vals):
    return jax.nn.silu(gate_vals) * up_vals


def right_trans(left, matrix):
    return lax.dot_general(
        left, matrix, (((1,), (1,)), ((), ())), preferred_element_type=jnp.float32
    )


def cross_rows(left, right):
    left_flat = left.reshape(-1, left.shape[-1])
    right_flat = right.reshape(-1, right.shape[-1])
    return lax.dot_general(
        left_flat, right_flat, (((0,), (0,)), ((), ())), preferred_element_type=jnp.float32
    )


def geometry(starts):
    row_count = starts.shape[0]
    local_rows = jnp.arange(row_count, dtype=jnp.int32)
    live_mask = starts <= local_rows
    position = jnp.where(live_mask, local_rows - starts, 0).astype(jnp.float32)
    frequency = rope_base ** (-2.0 * jnp.arange(HEAD_DIM // 2, dtype=jnp.float32) / HEAD_DIM)
    angles = position[:, None, None] * frequency[None, None, :]
    causal = local_rows[None, :] <= local_rows[:, None]
    inside = local_rows[None, :] >= starts[:, None]
    diagonal = local_rows[None, :] == local_rows[:, None]
    allowed = causal & inside | diagonal
    return (live_mask.astype(jnp.float32)[:, None], jnp.cos(angles), jnp.sin(angles), allowed)


def attention_block(normed_low, weights, cosine_table, sine_table, allowed):
    w_query, w_key, w_value = (weights[0], weights[1], weights[2])
    row_count = normed_low.shape[0]
    group_size = HEADS // KV_HEADS
    query_raw = jnp.dot(normed_low, w_query, preferred_element_type=jnp.float32)
    key_raw = jnp.dot(normed_low, w_key, preferred_element_type=jnp.float32)
    value_raw = jnp.dot(normed_low, w_value, preferred_element_type=jnp.float32)
    query_rot = rotate(
        query_raw.reshape(row_count, HEADS, HEAD_DIM), cosine_table, sine_table
    ).astype(jnp.bfloat16)
    key_rot = rotate(
        key_raw.reshape(row_count, KV_HEADS, HEAD_DIM), cosine_table, sine_table
    ).astype(jnp.bfloat16)
    value_heads = value_raw.astype(jnp.bfloat16).reshape(row_count, KV_HEADS, HEAD_DIM)
    grouped = query_rot.reshape(row_count, KV_HEADS, group_size, HEAD_DIM)
    scores = jnp.einsum(
        "qhgd,khd->hgqk", grouped, key_rot, preferred_element_type=jnp.float32
    ) * HEAD_DIM ** (-0.5)
    scores = jnp.where(allowed[None, None], scores, masked_score)
    row_peak = jnp.max(scores, axis=-1, keepdims=True)
    exp_scores = jnp.exp(scores - row_peak)
    probs_f32 = exp_scores / jnp.sum(exp_scores, axis=-1, keepdims=True)
    probs_low = probs_f32.astype(jnp.bfloat16)
    mixed_f32 = jnp.einsum(
        "hgqk,khd->qhgd", probs_low, value_heads, preferred_element_type=jnp.float32
    )
    mixed_low = mixed_f32.reshape(row_count, HEADS * HEAD_DIM).astype(jnp.bfloat16)
    return (mixed_low, (grouped, key_rot, value_heads, probs_f32, probs_low))


def layer_forward(source, weights, starts):
    w_query, w_key, w_value, w_output, w_gate, w_up, w_down, attn_gain, ffn_gain = weights
    live_rows, cosine_table, sine_table, allowed = geometry(starts)
    rows_f32 = source.astype(jnp.float32)
    normed_low = rms_scale(rows_f32, attn_gain.astype(jnp.float32)).astype(jnp.bfloat16)
    mixed_low, unused_saved = attention_block(
        normed_low, weights, cosine_table, sine_table, allowed
    )
    middle = rows_f32 + jnp.dot(mixed_low, w_output, preferred_element_type=jnp.float32)
    second_low = rms_scale(middle, ffn_gain.astype(jnp.float32)).astype(jnp.bfloat16)
    gate_vals = jnp.dot(second_low, w_gate, preferred_element_type=jnp.float32)
    up_vals = jnp.dot(second_low, w_up, preferred_element_type=jnp.float32)
    hidden_low = swiglu(gate_vals, up_vals).astype(jnp.bfloat16)
    result = (middle + jnp.dot(hidden_low, w_down, preferred_element_type=jnp.float32)) * live_rows
    return result.astype(jnp.bfloat16)


def layer_backward(source, weights, starts, upstream):
    w_query, w_key, w_value, w_output, w_gate, w_up, w_down, attn_gain, ffn_gain = weights
    live_rows, cosine_table, sine_table, allowed = geometry(starts)
    row_count = source.shape[0]
    group_size = HEADS // KV_HEADS
    score_scale = HEAD_DIM ** (-0.5)
    rows_f32 = source.astype(jnp.float32)
    first_normed, first_back = jax.vjp(rms_scale, rows_f32, attn_gain.astype(jnp.float32))
    normed_low = first_normed.astype(jnp.bfloat16)
    mixed_low, saved = attention_block(normed_low, weights, cosine_table, sine_table, allowed)
    grouped, key_rot, value_heads, probs_f32, probs_low = saved
    middle = rows_f32 + jnp.dot(mixed_low, w_output, preferred_element_type=jnp.float32)
    second_normed, second_back = jax.vjp(rms_scale, middle, ffn_gain.astype(jnp.float32))
    second_low = second_normed.astype(jnp.bfloat16)
    gate_vals = jnp.dot(second_low, w_gate, preferred_element_type=jnp.float32)
    up_vals = jnp.dot(second_low, w_up, preferred_element_type=jnp.float32)
    hidden_f32, hidden_back = jax.vjp(swiglu, gate_vals, up_vals)
    hidden_low = hidden_f32.astype(jnp.bfloat16)
    top_grad = upstream.astype(jnp.float32) * live_rows
    top_low = top_grad.astype(jnp.bfloat16)
    grad_hidden = right_trans(top_low, w_down)
    grad_gate_vals, grad_up_vals = hidden_back(grad_hidden)
    gate_low = grad_gate_vals.astype(jnp.bfloat16)
    up_low = grad_up_vals.astype(jnp.bfloat16)
    grad_second = right_trans(gate_low, w_gate) + right_trans(up_low, w_up)
    grad_middle_norm, grad_ffn_gain = second_back(grad_second)
    grad_middle = top_grad + grad_middle_norm
    middle_low = grad_middle.astype(jnp.bfloat16)
    grad_mixed = right_trans(middle_low, w_output).astype(jnp.bfloat16)
    grad_mixed = grad_mixed.reshape(row_count, KV_HEADS, group_size, HEAD_DIM)
    grad_probs = jnp.einsum(
        "qhgd,khd->hgqk", grad_mixed, value_heads, preferred_element_type=jnp.float32
    )
    grad_value_heads = jnp.einsum(
        "hgqk,qhgd->khd", probs_low, grad_mixed, preferred_element_type=jnp.float32
    )
    row_inner = jnp.sum(probs_f32 * grad_probs, axis=-1, keepdims=True)
    grad_scores = (probs_f32 * (grad_probs - row_inner)).astype(jnp.bfloat16)
    grad_query_rot = (
        jnp.einsum("hgqk,khd->qhgd", grad_scores, key_rot, preferred_element_type=jnp.float32)
        * score_scale
    )
    grad_key_rot = (
        jnp.einsum("hgqk,qhgd->khd", grad_scores, grouped, preferred_element_type=jnp.float32)
        * score_scale
    )
    grad_query_raw = rotate(
        grad_query_rot.reshape(row_count, HEADS, HEAD_DIM), cosine_table, -sine_table
    )
    grad_query_raw = grad_query_raw.reshape(row_count, HEADS * HEAD_DIM).astype(jnp.bfloat16)
    grad_key_raw = (
        rotate(grad_key_rot, cosine_table, -sine_table)
        .reshape(row_count, KV_HEADS * HEAD_DIM)
        .astype(jnp.bfloat16)
    )
    grad_value_raw = grad_value_heads.reshape(row_count, KV_HEADS * HEAD_DIM).astype(jnp.bfloat16)
    grad_normed = right_trans(grad_query_raw, w_query)
    grad_normed = grad_normed + right_trans(grad_key_raw, w_key)
    grad_normed = grad_normed + right_trans(grad_value_raw, w_value)
    grad_rows_norm, grad_attn_gain = first_back(grad_normed)
    grad_rows = grad_middle + grad_rows_norm
    operands = (
        normed_low,
        grad_query_raw,
        grad_key_raw,
        grad_value_raw,
        mixed_low,
        middle_low,
        second_low,
        gate_low,
        up_low,
        hidden_low,
        top_low,
    )
    return (grad_rows.astype(jnp.bfloat16), (grad_attn_gain, grad_ffn_gain), operands)


def weight_grads(operands):
    (
        normed_low,
        grad_query_raw,
        grad_key_raw,
        grad_value_raw,
        mixed_low,
        middle_low,
        second_low,
        gate_low,
        up_low,
        hidden_low,
        top_low,
    ) = operands
    return (
        cross_rows(normed_low, grad_query_raw),
        cross_rows(normed_low, grad_key_raw),
        cross_rows(normed_low, grad_value_raw),
        cross_rows(mixed_low, middle_low),
        cross_rows(second_low, gate_low),
        cross_rows(second_low, up_low),
        cross_rows(hidden_low, top_low),
    )


def flat_grads(grads, owner_count):
    pieces = [grad.reshape(owner_count, -1) for grad in grads]
    joined = jnp.concatenate(pieces, axis=1)
    width = joined.shape[1]
    padded = (width + 127) // 128 * 128
    return jnp.pad(joined, ((0, 0), (0, padded - width)))


def unflat_grads(flat_row, shard_shapes):
    flat_row = flat_row.reshape(-1)
    results = []
    offset = 0
    for shape in shard_shapes:
        length = 1
        for extent in shape:
            length = length * extent
        results.append(flat_row[offset : offset + length].reshape(shape))
        offset = offset + length
    return tuple(results)


def store_slot(buffer, rows_new, slot_idx, active):
    current = lax.dynamic_index_in_dim(buffer, slot_idx, 0, keepdims=False)
    chosen = jnp.where(active, rows_new, current)
    return lax.dynamic_update_index_in_dim(buffer, chosen, slot_idx, 0)


def body(
    inputs,
    starts,
    cotangent,
    w_query,
    w_key,
    w_value,
    w_output,
    w_gate,
    w_up,
    w_down,
    attn_gain,
    ffn_gain,
):
    section_idx = lax.axis_index("section")
    section_count = lax.axis_size("section")
    owner_count = lax.axis_size("dp")
    last_section = section_count - 1
    micro_count = inputs.shape[0]
    tick_count = micro_count + section_count - 1
    shard_list = (w_query, w_key, w_value, w_output, w_gate, w_up, w_down, attn_gain, ffn_gain)
    shard_shapes = tuple((piece.shape for piece in shard_list))
    gathered = (
        lax.all_gather(w_query, "dp", axis=1, tiled=True),
        lax.all_gather(w_key, "dp", axis=1, tiled=True),
        lax.all_gather(w_value, "dp", axis=1, tiled=True),
        lax.all_gather(w_output, "dp", axis=1, tiled=True),
        lax.all_gather(w_gate, "dp", axis=1, tiled=True),
        lax.all_gather(w_up, "dp", axis=1, tiled=True),
        lax.all_gather(w_down, "dp", axis=1, tiled=True),
        lax.all_gather(attn_gain, "dp", axis=1, tiled=True),
        lax.all_gather(ffn_gain, "dp", axis=1, tiled=True),
    )
    weights = tuple((piece[0] for piece in gathered))
    blank_rows = jnp.zeros(inputs.shape[1:], jnp.bfloat16)
    kept_in = jnp.zeros(inputs.shape, jnp.bfloat16)
    section_acts = jnp.zeros(inputs.shape, jnp.bfloat16)
    received = blank_rows
    for moment in range(tick_count):
        slot_raw = moment - section_idx
        active = (slot_raw >= 0) & (slot_raw < micro_count)
        slot_idx = jnp.clip(slot_raw, 0, micro_count - 1)
        feed_rows = jnp.where(section_idx == 0, inputs[min(moment, micro_count - 1)], received)
        starts_now = starts[slot_idx]
        produced = lax.cond(
            active, partial(layer_forward, feed_rows, weights, starts_now), lambda: blank_rows
        )
        kept_in = store_slot(kept_in, feed_rows, slot_idx, active)
        section_acts = store_slot(section_acts, produced, slot_idx, active)
        if moment + 1 < tick_count:
            received = from_behind(produced, "section", 1)
    regathered = (
        lax.all_gather(w_query, "dp", axis=1, tiled=True),
        lax.all_gather(w_key, "dp", axis=1, tiled=True),
        lax.all_gather(w_value, "dp", axis=1, tiled=True),
        lax.all_gather(w_output, "dp", axis=1, tiled=True),
        lax.all_gather(w_gate, "dp", axis=1, tiled=True),
        lax.all_gather(w_up, "dp", axis=1, tiled=True),
        lax.all_gather(w_down, "dp", axis=1, tiled=True),
        lax.all_gather(attn_gain, "dp", axis=1, tiled=True),
        lax.all_gather(ffn_gain, "dp", axis=1, tiled=True),
    )
    back_weights = tuple((piece[0] for piece in regathered))
    row_count = inputs.shape[1]
    operand_widths = (D, QD, KVD, KVD, QD, D, D, FF, FF, FF, D)
    blank_operands = tuple(
        (jnp.zeros((row_count, width), jnp.bfloat16) for width in operand_widths)
    )
    blank_gains = (
        jnp.zeros(back_weights[7].shape, jnp.float32),
        jnp.zeros(back_weights[8].shape, jnp.float32),
    )
    operand_store = tuple(
        (jnp.zeros((micro_count, row_count, width), jnp.bfloat16) for width in operand_widths)
    )
    gain_totals = blank_gains
    shard_totals = tuple((jnp.zeros(shape, jnp.float32) for shape in shard_shapes))
    input_grads = jnp.zeros(inputs.shape, jnp.bfloat16)
    returned = blank_rows
    for moment in range(tick_count):
        slot_raw = moment - (last_section - section_idx)
        active = (slot_raw >= 0) & (slot_raw < micro_count)
        slot_idx = jnp.clip(slot_raw, 0, micro_count - 1)
        upstream = jnp.where(
            section_idx == last_section, cotangent[min(moment, micro_count - 1)], returned
        )
        source = lax.dynamic_index_in_dim(kept_in, slot_idx, 0, keepdims=False)
        starts_now = starts[slot_idx]

        def run_keep():
            return layer_backward(source, back_weights, starts_now, upstream)

        def skip_keep():
            return (blank_rows, blank_gains, blank_operands)

        grad_rows, gain_grads, operands = lax.cond(active, run_keep, skip_keep)
        gain_totals = tuple(
            (old_sum + new_sum for old_sum, new_sum in zip(gain_totals, gain_grads))
        )
        operand_store = tuple(
            (
                store_slot(buffer, member, slot_idx, active)
                for buffer, member in zip(operand_store, operands)
            )
        )
        input_grads = store_slot(input_grads, grad_rows, slot_idx, active)
        if moment + 1 < tick_count:
            returned = from_behind(grad_rows, "section", -1)
    totals = weight_grads(operand_store) + gain_totals
    scattered = lax.psum_scatter(
        flat_grads(totals, owner_count), "dp", scatter_dimension=0, tiled=True
    )
    shard_totals = unflat_grads(scattered, shard_shapes)
    return (section_acts[None], input_grads[None]) + tuple(shard_totals)


def solution(mesh):
    return jax.shard_map(
        body,
        mesh=mesh,
        in_specs=(
            P(None, "dp", None),
            P(None, "dp"),
            P(None, "dp", None),
            P("section", "dp", None),
            P("section", "dp", None),
            P("section", "dp", None),
            P("section", "dp", None),
            P("section", "dp", None),
            P("section", "dp", None),
            P("section", "dp", None),
            P("section", "dp"),
            P("section", "dp"),
        ),
        out_specs=(
            P("section", None, "dp", None),
            P("section", None, "dp", None),
            P("section", "dp", None),
            P("section", "dp", None),
            P("section", "dp", None),
            P("section", "dp", None),
            P("section", "dp", None),
            P("section", "dp", None),
            P("section", "dp", None),
            P("section", "dp"),
            P("section", "dp"),
        ),
        check_vma=False,
    )
```

profile of v0, /device:TPU:0, one launch (start us, length us, event | category | flops | bytes accessed | tf_op | source)
XLA Modules:
  0.0 1488.7 jit_solution(15037251605952661277)
XLA Ops:
  15.2 188.1 %all_gather.37 = bf16[1,960,320]{2,0,1:T(2,128)(2,1)S(1)} all-gather(bf16[1,15,320]{2,0,1:T(2,128)(2,1)S(1)} %copy.462), channel_id=1, replica_groups=mesh['section'=2,'dp'=64] {'dp'}, dimensions={1}, use_global_device_ids=true | all-gather | bytes 624000 | tf_op jit(solution)/shard_map/all_gather | solution.py:276
  206.3 183.7 %all_gather.38 = bf16[1,960,320]{2,0,1:T(2,128)(2,1)S(1)} all-gather(bf16[1,15,320]{2,0,1:T(2,128)(2,1)S(1)} %copy.464), channel_id=1, replica_groups=mesh['section'=2,'dp'=64] {'dp'}, dimensions={1}, use_global_device_ids=true | all-gather | bytes 624000 | tf_op jit(solution)/shard_map/all_gather | solution.py:275
  394.3 173.6 %all-reduce.4 = (bf16[960]{0:T(1024)(128)(2,1)S(1)}, bf16[960]{0:T(1024)(128)(2,1)S(1)}) all-reduce(bf16[960]{0:T(1024)(128)(2,1)S(1)} %dynamic-update-slice, bf16[960]{0:T(1024)(128)(2,1)S(1)} %dynamic-update-slice.1), channel_id=1, replica_groups=mesh['section'=2,'dp'=64] {'dp'}, use_global_device_ids=true, to_apply=%add.1 | all-reduce | flops 1920 | bytes 7680 | tf_op jit(solution)/shard_map/squeeze | solution.py:284
  568.6 2.9 copy.614
  571.5 4.2 copy.613
  575.7 7.3 copy.612
  583.0 7.2 copy.611
  590.9 39.5 %conditional.6 = (bf16[64,960]{1,0:T(8,128)(2,1)}) conditional(s32[]{:T(128)} %convert_element_type.647, () %tuple.72, (pred[]{:T(512)}, bf16[1,64,960]{2,1,0:T(8,128)(2,1)}, bf16[64,960]{1,0:T(8,128)(2,1)}, bf16[960]{0:T(1024)(128)(2,1)S(1)}, bf16[960,320]{0,1:T(8,128)(2,1)S(1)}, /*index=5*/s32[2,64]{1,0:T(2,128)S(1)}, s32[]{:T(128)}, ...), branch_computations={%region_0.1_spmd, %region_1.6_spmd} | conditional | flops 1286292992 | bytes 26960564 | solution.py:295
  619.2 4.3 fusion.22
  623.5 6.9 fusion.9
  634.6 39.3 %conditional.7 = (bf16[64,960]{1,0:T(8,128)(2,1)}) conditional(s32[]{:T(128)} %convert_element_type.648, () %tuple.74, (bf16[64,960]{1,0:T(8,128)(2,1)}, bf16[960]{0:T(1024)(128)(2,1)S(1)}, bf16[960,320]{0,1:T(8,128)(2,1)S(1)}, s32[2,64]{1,0:T(2,128)S(1)}, s32[]{:T(128)}, /*index=5*/bf16[960,320]{0,1:T(8,128)(2,1)S(1)}, ...), branch_computations={%region_6.7_spmd, %region_7.12_spmd} | conditional | flops 1286231552 | bytes 26223256 | solution.py:295
  662.8 4.3 fusion.84
  667.1 6.9 fusion.71
  674.0 3.0 collective-permute-start.1
  680.9 9.5 conditional.9
  711.4 38.0 %collective-permute-done.2 = bf16[64,960]{1,0:T(8,128)(2,1)} collective-permute-done((bf16[64,960]{1,0:T(8,128)(2,1)}, bf16[64,960]{1,0:T(8,128)(2,1)}, u32[]{:S(2)}, u32[]{:S(2)}) %collective-permute-start.2) | collective-permute-done | bytes 122912 | tf_op jit(solution)/shard_map/ppermute | solution.py:22
  749.4 65.9 %conditional.10 = (bf16[64,960]{1,0:T(8,128)(2,1)}, f32[960]{0:T(1024)}, f32[960]{0:T(1024)}, bf16[64,960]{1,0:T(8,128)(2,1)}, bf16[64,320]{0,1:T(8,128)(2,1)}, ...) conditional(s32[]{:T(128)} %convert_element_type.651, () %tuple.80, ...), branch_computations={%region_29.30_spmd, %region_30.40_spmd} | conditional | flops 2275088896 | bytes 119995208 | solution.py:346
  758.5 2.9 copy.479
  776.6 3.8 fusion.371
  780.5 2.8 fusion.370
  783.3 3.0 multiply_convert_fusion.16
  788.9 3.3 multiply_reduce_fusion.8
  855.5 65.6 %conditional.11 = (bf16[64,960]{1,0:T(8,128)(2,1)}, f32[960]{0:T(1024)}, f32[960]{0:T(1024)}, bf16[64,960]{1,0:T(8,128)(2,1)}, bf16[64,320]{0,1:T(8,128)(2,1)}, ...) conditional(s32[]{:T(128)} %convert_element_type.652, () %tuple.82, ...), branch_computations={%region_40.41_spmd, %region_41.51_spmd} | conditional | flops 2275088896 | bytes 119995208 | solution.py:346
  882.3 3.8 fusion.375
  886.2 2.8 fusion.374
  889.0 2.9 multiply_convert_fusion.20
  894.6 3.3 multiply_reduce_fusion.12
  924.4 3.6 convolution_bitcast_fusion.13
  928.1 5.3 reshape.1296
  936.0 2.9 reshape.1297
  941.5 2.9 reshape.1298
  948.8 5.4 reshape.1299
  956.9 6.1 convolution_bitcast_fusion.11
  963.0 11.9 reshape.1300
  976.0 6.1 convolution_bitcast_fusion.10
  982.1 12.0 reshape.1301
  996.1 5.5 convolution_bitcast_fusion.9
  1001.6 12.2 reshape.1302
  1014.9 11.4 dynamic-update-slice.2
  1026.3 6.4 dynamic-update-slice.3
  1032.7 6.2 dynamic-update-slice.4
  1039.0 12.3 dynamic-update-slice.5
  1051.3 8.6 constant_dynamic-update-slice_fusion.8
  1059.9 4.3 constant_dynamic-update-slice_fusion.7
  1064.3 8.3 constant_dynamic-update-slice_fusion.6
  1075.4 27.2 %pad.4 = f32[64,153728]{1,0:T(8,128)} pad(f32[64,153630]{1,0:T(8,128)} %dynamic-update-slice.10, f32[]{:T(128)} %constant.520.clone.1), padding=0_0x0_98 | pad | bytes 78683648 | tf_op jit(solution)/shard_map/jit(_pad)/pad | solution.py:229
  1107.5 360.2 %all-reduce.7.cloned.1.call-done = f32[64,153728]{1,0:T(8,128)} async-done(((f32[64,153728]{1,0:T(8,128)}), f32[64,153728]{1,0:T(8,128)}) %all-reduce.7.cloned.1.call-update) | async-done | bytes 39354384
  1474.5 4.4 dynamic-slice_reduce_fusion
  (552 shorter events, 288.8 us)
Async XLA Ops:
  7.2 385.2 %copy-start.120 = (u32[128]{0:T(128)S(1)}, u32[128]{0:T(128)}, u32[]{:S(2)}) copy-start(u32[128]{0:T(128)} %constant.534) | copy-start | bytes 1540
  7.2 386.6 %copy-start.126 = (bf16[1,15]{1,0:T(2,128)(2,1)S(1)}, bf16[1,15]{1,0:T(2,128)(2,1)}, u32[]{:S(2)}) copy-start(bf16[1,15]{1,0:T(2,128)(2,1)} %param.34) | copy-start | bytes 94
  7.2 386.9 %copy-start.127 = (bf16[1,15]{1,0:T(2,128)(2,1)S(1)}, bf16[1,15]{1,0:T(2,128)(2,1)}, u32[]{:S(2)}) copy-start(bf16[1,15]{1,0:T(2,128)(2,1)} %param.35) | copy-start | bytes 94
  7.2 560.7 %copy-start.70 = (bf16[2,64,960]{2,1,0:T(8,128)(2,1)S(1)}, bf16[2,64,960]{2,1,0:T(8,128)(2,1)}, u32[]{:S(2)}) copy-start(bf16[2,64,960]{2,1,0:T(8,128)(2,1)} %param.24) | copy-start | bytes 737284
  7.2 561.4 %all-gather.6.cloned.1.call-start = ((), (), s32[]{:S(2)}) async-start(), calls=%async_computation | async-start | bytes 3993600 | tf_op jit(solution)/shard_map/all_gather | solution.py:274
  8.8 562.8 %all-gather.8.cloned.1.call-start = ((), (), s32[]{:S(2)}) async-start(), calls=%async_computation.1 | async-start | bytes 3993600 | tf_op jit(solution)/shard_map/all_gather | solution.py:277
  10.3 565.5 %all-gather.10.cloned.1.call-start = ((), (), s32[]{:S(2)}) async-start(), calls=%async_computation.2 | async-start | bytes 9984000 | tf_op jit(solution)/shard_map/all_gather | solution.py:278
  12.0 571.0 %all-gather.12.cloned.1.call-start = ((), (), s32[]{:S(2)}) async-start(), calls=%async_computation.3 | async-start | bytes 9984000 | tf_op jit(solution)/shard_map/all_gather | solution.py:279
  13.8 576.5 %all-gather.14.cloned.1.call-start = ((), (), s32[]{:S(2)}) async-start(), calls=%async_computation.4 | async-start | bytes 5324800 | tf_op jit(solution)/shard_map/all_gather | solution.py:280
  14.4 1453.3 %all-reduce.7.cloned.1.call-start = ((), (), s32[]{:S(2)}) async-start(), calls=%async_computation.5 | async-start | bytes 78708736
  205.6 474.7 %copy-start.4 = (bf16[1,960,320]{1,2,0:T(8,128)(2,1)}, bf16[1,960,320]{1,2,0:T(8,128)(2,1)S(1)}, u32[]{:S(2)}) copy-start(bf16[1,960,320]{1,2,0:T(8,128)(2,1)S(1)} %copy.463) | copy-start | bytes 1843204
  392.4 287.9 %copy-start.14 = (bf16[1,960,320]{1,2,0:T(8,128)(2,1)}, bf16[1,960,320]{1,2,0:T(8,128)(2,1)S(1)}, u32[]{:S(2)}) copy-start(bf16[1,960,320]{1,2,0:T(8,128)(2,1)S(1)} %copy.465) | copy-start | bytes 1843204
  567.9 112.4 %copy-start.94 = (bf16[960]{0:T(1024)(128)(2,1)}, bf16[960]{0:T(1024)(128)(2,1)S(1)}, u32[]{:S(2)}) copy-start(bf16[960]{0:T(1024)(128)(2,1)S(1)} %get-tuple-element.1183) | copy-start | bytes 5764
  567.9 112.4 %copy-start.98 = (bf16[960]{0:T(1024)(128)(2,1)}, bf16[960]{0:T(1024)(128)(2,1)S(1)}, u32[]{:S(2)}) copy-start(bf16[960]{0:T(1024)(128)(2,1)S(1)} %get-tuple-element.1184) | copy-start | bytes 5764
  630.4 2.6 collective-permute-start
  674.0 4.6 collective-permute-start.1
  690.4 59.0 %collective-permute-start.2 = (bf16[64,960]{1,0:T(8,128)(2,1)}, bf16[64,960]{1,0:T(8,128)(2,1)}, u32[]{:S(2)}, u32[]{:S(2)}) collective-permute-start(bf16[64,960]{1,0:T(8,128)(2,1)} %get-tuple-element.623), channel_id=1, source_target_pairs={{64,0},{65,1},{66,2},{67,3},{68,4},{69,5},{70,6},{71,7},{72,8},{73... | collective-permute-start | bytes 368648 | tf_op jit(solution)/shard_map/ppermute | solution.py:22
  695.4 54.0 %copy-start.5 = (bf16[1,960,320]{1,2,0:T(8,128)(2,1)S(1)}, bf16[1,960,320]{1,2,0:T(8,128)(2,1)}, u32[]{:S(2)}) copy-start(bf16[1,960,320]{1,2,0:T(8,128)(2,1)} %copy-done.4) | copy-start | bytes 1843204
  695.4 54.0 %copy-start.15 = (bf16[1,960,320]{1,2,0:T(8,128)(2,1)S(1)}, bf16[1,960,320]{1,2,0:T(8,128)(2,1)}, u32[]{:S(2)}) copy-start(bf16[1,960,320]{1,2,0:T(8,128)(2,1)} %copy-done.14) | copy-start | bytes 1843204
  695.4 54.0 %copy-start.95 = (bf16[960]{0:T(1024)(128)(2,1)S(1)}, bf16[960]{0:T(1024)(128)(2,1)}, u32[]{:S(2)}) copy-start(bf16[960]{0:T(1024)(128)(2,1)} %copy-done.94) | copy-start | bytes 5764
  695.4 54.0 %copy-start.108 = (s32[2,64]{1,0:T(2,128)S(1)}, s32[2,64]{1,0:T(2,128)}, u32[]{:S(2)}) copy-start(s32[2,64]{1,0:T(2,128)} %param.25) | copy-start | bytes 1540
  749.4 15.7 %copy-start.10 = (bf16[960,320]{0,1:T(8,128)(2,1)}, bf16[960,320]{0,1:T(8,128)(2,1)S(1)}, u32[]{:S(2)}) copy-start(bf16[960,320]{0,1:T(8,128)(2,1)S(1)} %get-tuple-element.1128) | copy-start | bytes 1843204 | tf_op jit(solution)/shard_map/cond
  749.4 15.7 %copy-start.20 = (bf16[960,320]{0,1:T(8,128)(2,1)}, bf16[960,320]{0,1:T(8,128)(2,1)S(1)}, u32[]{:S(2)}) copy-start(bf16[960,320]{0,1:T(8,128)(2,1)S(1)} %get-tuple-element.549) | copy-start | bytes 1843204 | tf_op jit(solution)/shard_map/cond
  768.1 12.4 slice-start.14
  815.3 40.1 %collective-permute-start.3 = (bf16[64,960]{1,0:T(8,128)(2,1)}, bf16[64,960]{1,0:T(8,128)(2,1)}, u32[]{:S(2)}, u32[]{:S(2)}) collective-permute-start(bf16[64,960]{1,0:T(8,128)(2,1)} %get-tuple-element.624), channel_id=1, source_target_pairs={{64,0},{65,1},{66,2},{67,3},{68,4},{69,5},{70,6},{71,7},{72,8},{73... | collective-permute-start | bytes 368648 | tf_op jit(solution)/shard_map/ppermute | solution.py:22
  818.5 37.0 %copy-start.6 = (bf16[1,960,320]{1,2,0:T(8,128)(2,1)S(1)}, bf16[1,960,320]{1,2,0:T(8,128)(2,1)}, u32[]{:S(2)}) copy-start(bf16[1,960,320]{1,2,0:T(8,128)(2,1)} %copy-done.4) | copy-start | bytes 1843204
  818.5 37.0 %copy-start.16 = (bf16[1,960,320]{1,2,0:T(8,128)(2,1)S(1)}, bf16[1,960,320]{1,2,0:T(8,128)(2,1)}, u32[]{:S(2)}) copy-start(bf16[1,960,320]{1,2,0:T(8,128)(2,1)} %copy-done.14) | copy-start | bytes 1843204
  818.5 37.0 %copy-start.96 = (bf16[960]{0:T(1024)(128)(2,1)S(1)}, bf16[960]{0:T(1024)(128)(2,1)}, u32[]{:S(2)}) copy-start(bf16[960]{0:T(1024)(128)(2,1)} %copy-done.94) | copy-start | bytes 5764
  818.5 37.0 %copy-start.109 = (s32[2,64]{1,0:T(2,128)S(1)}, s32[2,64]{1,0:T(2,128)}, u32[]{:S(2)}) copy-start(s32[2,64]{1,0:T(2,128)} %param.25) | copy-start | bytes 1540
  832.3 17.9 %copy-start.68 = (bf16[2,64,320]{2,1,0:T(8,128)(2,1)S(1)}, bf16[2,64,320]{2,1,0:T(8,128)(2,1)}, u32[]{:S(2)}) copy-start(bf16[2,64,320]{2,1,0:T(8,128)(2,1)} %constant_dynamic-update-slice_fusion.1) | copy-start | bytes 245764
  855.5 15.3 %copy-start.12 = (bf16[960,320]{0,1:T(8,128)(2,1)}, bf16[960,320]{0,1:T(8,128)(2,1)S(1)}, u32[]{:S(2)}) copy-start(bf16[960,320]{0,1:T(8,128)(2,1)S(1)} %get-tuple-element.1143) | copy-start | bytes 1843204 | tf_op jit(solution)/shard_map/cond
  855.5 15.3 %copy-start.22 = (bf16[960,320]{0,1:T(8,128)(2,1)}, bf16[960,320]{0,1:T(8,128)(2,1)S(1)}, u32[]{:S(2)}) copy-start(bf16[960,320]{0,1:T(8,128)(2,1)S(1)} %get-tuple-element.564) | copy-start | bytes 1843204 | tf_op jit(solution)/shard_map/cond
  873.8 12.4 slice-start.16
  928.0 10.9 copy-start.77
  928.0 11.9 copy-start.69
  934.3 10.0 copy-start.46
  934.3 10.0 copy-start.75
  934.5 10.8 copy-start.44
  934.5 10.8 copy-start.72
  963.0 12.0 copy-start.31
  963.0 12.0 copy-start.61
  982.1 12.0 copy-start.25
  982.1 12.0 copy-start.59
  982.1 13.0 copy-start.48
  982.1 13.0 copy-start.73
  1013.8 12.5 copy-start.32
  1039.0 20.9 %slice-start.18 = ((s8[9830400]{0:T(1024)(128)(4,1)}), s8[1441792]{0:T(1024)(128)(4,1)S(1)}, s32[]{:S(2)}) async-start(s8[9830400]{0:T(1024)(128)(4,1)} %bitcast.940), calls=%async_computation.24 | async-start | bytes 2883584
  1107.5 374.1 %copy-start.83 = (bf16[1,2,64,960]{3,2,1,0:T(8,128)(2,1)}, bf16[1,2,64,960]{3,2,1,0:T(8,128)(2,1)S(1)}, u32[]{:S(2)}) copy-start(bf16[1,2,64,960]{3,2,1,0:T(8,128)(2,1)S(1)} %get-tuple-element.1332) | copy-start | bytes 737284
  (82 other events, 355.4 us)
Sparse Core Ops, SparseCore 0:
  11.4 71.4 all-gather.5
  86.2 67.3 all-gather.7
  157.0 83.9 all-gather.9
  244.3 85.3 all-gather.11
  332.5 69.7 all-gather.13
  1102.8 364.8 all-reduce.6
where the time goes:
time: 1500 us; the launch traced here: 1490 us
  blocking collectives  545 us (36%)
  waiting for transfers between devices  400 us (27%)
  local copies, waits for them, and re-layouts  291 us (19%)
  matrix products  152 us (10%)
  other arithmetic  75 us (5%)
  between operations  15.9 us (1%)
    unnamed x7, waiting for transfers between devices  361 us
    all_gather x1, blocking collectives, body(): lax.all_gather(w_value, 'dp', axis=1, tiled=True)  188 us
    all_gather x1, blocking collectives, body(): lax.all_gather(w_key, 'dp', axis=1, tiled=True)  184 us
    squeeze x1, blocking collectives, body(): weights = tuple((piece[0] for piece in gathered))  174 us
    unnamed x147, local copies, waits for them, and re-layouts  94.3 us
    reshape x9, local copies, waits for them, and re-layouts, flat_grads(): pieces = [grad.reshape(owner_count, -1) for grad in grads]  52.9 us
    ppermute x4, waiting for transfers between devices, from_behind(): lax.ppermute(value, axis, [(source, source + steps) for source in range(f...  38.7 us
    dynamic_slice x30, local copies, waits for them, and re-layouts, store_slot(): current = lax.dynamic_index_in_dim(buffer, slot_idx, 0, keepdims=False)  31.6 us
  transfers between devices with their start and end apart: 10, of which 3 were waited for; matrix products, arithmetic and copies ran while one was open for 6% of the time, Pallas kernels for 0%

commit v1 on v0

--- a/solution.py
+++ b/solution.py
@@ -14,6 +14,14 @@
 norm_eps = 1e-05
 masked_score = -1e30
 rope_base = 10000.0
+
+
+def gather_by_exchange(value, axis, dim):
+    devices = lax.axis_size(axis)
+    repeats = [devices if d == dim else 1 for d in range(value.ndim)]
+    return lax.all_to_all(
+        jnp.tile(value, repeats), axis, split_axis=dim, concat_axis=dim, tiled=True
+    )
 
 
 def from_behind(value, axis, steps):
@@ -272,7 +280,7 @@
     shard_shapes = tuple((piece.shape for piece in shard_list))
     gathered = (
         lax.all_gather(w_query, "dp", axis=1, tiled=True),
-        lax.all_gather(w_key, "dp", axis=1, tiled=True),
+        gather_by_exchange(w_key, "dp", 1),
         lax.all_gather(w_value, "dp", axis=1, tiled=True),
         lax.all_gather(w_output, "dp", axis=1, tiled=True),
         lax.all_gather(w_gate, "dp", axis=1, tiled=True),

time: 1500 us -> 1530 us (1.020)
  blocking collectives: 545 us -> 565 us
    all_gather x1, blocking collectives: 184 us -> 203 us  [body(): lax.all_gather(w_key, 'dp', axis=1, tiled=True)]
    unnamed x147 -> x152, local copies, waits for them, and re-layouts: 94.3 us -> 96.7 us
  transfers between devices with their start and end apart: 10 -> 11, of which waited for: 3 -> 2; matrix products, arithmetic and copies ran while one was open for 6% -> 7% of each run, Pallas kernels for 0% -> 0%
where the time goes in v1:
time: 1530 us; the launch traced here: 1510 us
  blocking collectives  565 us (37%)
  waiting for transfers between devices  393 us (26%)
  local copies, waits for them, and re-layouts  293 us (19%)
  matrix products  152 us (10%)
  other arithmetic  75.1 us (5%)
  starting transfers between devices  17.7 us (1%)
  between operations  16.1 us (1%)
    unnamed x7, waiting for transfers between devices  360 us
    all_gather x1, blocking collectives, body(): lax.all_gather(w_key, 'dp', axis=1, tiled=True)  203 us
    all_gather x1, blocking collectives, body(): lax.all_gather(w_value, 'dp', axis=1, tiled=True)  189 us
    squeeze x1, blocking collectives, body(): weights = tuple((piece[0] for piece in gathered))  173 us
    unnamed x152, local copies, waits for them, and re-layouts  96.7 us
    reshape x9, local copies, waits for them, and re-layouts, flat_grads(): pieces = [grad.reshape(owner_count, -1) for grad in grads]  52.9 us
    ppermute x4, waiting for transfers between devices, from_behind(): lax.ppermute(value, axis, [(source, source + steps) for source in range(f...  32.8 us
    dynamic_slice x30, local copies, waits for them, and re-layouts, store_slot(): current = lax.dynamic_index_in_dim(buffer, slot_idx, 0, keepdims=False)  30.8 us
  transfers between devices with their start and end apart: 11, of which 2 were waited for; matrix products, arithmetic and copies ran while one was open for 7% of the time, Pallas kernels for 0%

profile of v1, /device:TPU:0, one launch (start us, length us, event | category | flops | bytes accessed | tf_op | source)
XLA Modules:
  0.0 1513.0 jit_solution(13037895778211483063)
XLA Ops:
  16.1 5.4 reduce.10
  23.6 11.5 all-to-all-start
  35.8 189.2 %all_gather.36 = bf16[1,960,320]{2,0,1:T(2,128)(2,1)S(1)} all-gather(bf16[1,15,320]{2,0,1:T(2,128)(2,1)S(1)} %copy.454), channel_id=1, replica_groups=mesh['section'=2,'dp'=64] {'dp'}, dimensions={1}, use_global_device_ids=true | all-gather | bytes 624000 | tf_op jit(solution)/shard_map/all_gather | solution.py:284
  229.3 173.2 %all-reduce.4 = (bf16[960]{0:T(1024)(128)(2,1)S(1)}, bf16[960]{0:T(1024)(128)(2,1)S(1)}) all-reduce(bf16[960]{0:T(1024)(128)(2,1)S(1)} %dynamic-update-slice, bf16[960]{0:T(1024)(128)(2,1)S(1)} %dynamic-update-slice.1), channel_id=1, replica_groups=mesh['section'=2,'dp'=64] {'dp'}, use_global_device_ids=true, to_apply=%add.1 | all-reduce | flops 1920 | bytes 7680 | tf_op jit(solution)/shard_map/squeeze | solution.py:292
  407.1 3.1 copy.608
  410.3 4.2 copy.607
  414.5 7.3 copy.606
  421.7 7.2 copy.605
  429.7 38.8 %conditional.6 = (bf16[64,960]{1,0:T(8,128)(2,1)}) conditional(s32[]{:T(128)} %convert_element_type.647, () %tuple.72, (pred[]{:T(512)}, bf16[1,64,960]{2,1,0:T(8,128)(2,1)}, bf16[64,960]{1,0:T(8,128)(2,1)}, bf16[960]{0:T(1024)(128)(2,1)S(1)}, bf16[960,320]{0,1:T(8,128)(2,1)S(1)}, /*index=5*/s32[2,64]{1,0:T(2,128)S(1)}, s32[]{:T(128)}, ...), branch_computations={%region_0.1_spmd, %region_1.6_spmd} | conditional | flops 1286292992 | bytes 26960564 | solution.py:303
  457.3 4.3 fusion.22
  461.5 6.9 fusion.9
  470.4 202.9 %all_gather.43 = bf16[1,960,320]{2,0,1:T(2,128)(2,1)} all-gather(bf16[1,15,320]{2,0,1:T(2,128)(2,1)} %copy.468), channel_id=1, replica_groups=mesh['section'=2,'dp'=64] {'dp'}, dimensions={1}, use_global_device_ids=true | all-gather | bytes 624000 | tf_op jit(solution)/shard_map/all_gather | solution.py:312
  675.0 31.9 %conditional.7 = (bf16[64,960]{1,0:T(8,128)(2,1)}) conditional(s32[]{:T(128)} %convert_element_type.648, () %tuple.74, (bf16[64,960]{1,0:T(8,128)(2,1)}, bf16[960]{0:T(1024)(128)(2,1)S(1)}, bf16[960,320]{0,1:T(8,128)(2,1)S(1)}, s32[2,64]{1,0:T(2,128)S(1)}, s32[]{:T(128)}, /*index=5*/bf16[960,320]{0,1:T(8,128)(2,1)S(1)}, ...), branch_computations={%region_6.7_spmd, %region_7.12_spmd} | conditional | flops 1286231552 | bytes 26714804 | solution.py:303
  696.8 3.4 fusion.84
  700.2 6.7 fusion.71
  709.7 4.6 copy.469
  716.6 9.3 conditional.9
  744.0 32.8 %collective-permute-done.2 = bf16[64,960]{1,0:T(8,128)(2,1)} collective-permute-done((bf16[64,960]{1,0:T(8,128)(2,1)}, bf16[64,960]{1,0:T(8,128)(2,1)}, u32[]{:S(2)}, u32[]{:S(2)}) %collective-permute-start.2) | collective-permute-done | bytes 122912 | tf_op jit(solution)/shard_map/ppermute | solution.py:30
  776.9 64.6 %conditional.10 = (bf16[64,960]{1,0:T(8,128)(2,1)}, f32[960]{0:T(1024)}, f32[960]{0:T(1024)}, bf16[64,960]{1,0:T(8,128)(2,1)}, bf16[64,320]{0,1:T(8,128)(2,1)}, ...) conditional(s32[]{:T(128)} %convert_element_type.651, () %tuple.80, ...), branch_computations={%region_29.30_spmd, %region_30.40_spmd} | conditional | flops 2275088896 | bytes 115481488 | solution.py:354
  786.9 2.9 copy.473
  804.9 3.8 fusion.371
  811.6 3.0 multiply_convert_fusion.16
  817.2 3.3 multiply_reduce_fusion.8
  880.7 64.5 %conditional.11 = (bf16[64,960]{1,0:T(8,128)(2,1)}, f32[960]{0:T(1024)}, f32[960]{0:T(1024)}, bf16[64,960]{1,0:T(8,128)(2,1)}, bf16[64,320]{0,1:T(8,128)(2,1)}, ...) conditional(s32[]{:T(128)} %convert_element_type.652, () %tuple.82, ...), branch_computations={%region_40.41_spmd, %region_41.51_spmd} | conditional | flops 2275088896 | bytes 115481488 | solution.py:354
  908.6 3.8 fusion.375
  915.2 3.0 multiply_convert_fusion.20
  920.9 3.3 multiply_reduce_fusion.12
  948.6 3.6 convolution_bitcast_fusion.13
  952.2 5.3 reshape.1302
  960.2 2.9 reshape.1303
  965.6 2.8 reshape.1304
  973.0 5.4 reshape.1305
  981.0 6.1 convolution_bitcast_fusion.11
  987.1 12.0 reshape.1306
  1000.2 6.1 convolution_bitcast_fusion.10
  1006.3 12.0 reshape.1307
  1020.3 5.5 convolution_bitcast_fusion.9
  1025.8 12.2 reshape.1308
  1039.1 11.4 dynamic-update-slice.2
  1050.5 6.5 dynamic-update-slice.3
  1057.0 6.3 dynamic-update-slice.4
  1063.3 12.3 dynamic-update-slice.5
  1075.6 8.6 constant_dynamic-update-slice_fusion.8
  1084.2 4.3 constant_dynamic-update-slice_fusion.7
  1088.5 8.4 constant_dynamic-update-slice_fusion.6
  1099.7 27.1 %pad.4 = f32[64,153728]{1,0:T(8,128)} pad(f32[64,153630]{1,0:T(8,128)} %dynamic-update-slice.10, f32[]{:T(128)} %constant.520.clone.1), padding=0_0x0_98 | pad | bytes 78683648 | tf_op jit(solution)/shard_map/jit(_pad)/pad | solution.py:237
  1132.4 359.4 %all-reduce.7.cloned.1.call-done = f32[64,153728]{1,0:T(8,128)} async-done(((f32[64,153728]{1,0:T(8,128)}), f32[64,153728]{1,0:T(8,128)}) %all-reduce.7.cloned.1.call-update) | async-done | bytes 39354384
  1498.6 4.4 dynamic-slice_reduce_fusion
  (573 shorter events, 287.0 us)
Async XLA Ops:
  7.2 28.0 %copy-start.97 = (bf16[1,15,320]{2,1,0:T(8,128)(2,1)S(1)}, bf16[1,15,320]{2,1,0:T(8,128)(2,1)}, u32[]{:S(2)}) copy-start(bf16[1,15,320]{2,1,0:T(8,128)(2,1)} %param.28) | copy-start | bytes 28804
  7.2 28.6 %copy-start.104 = (bf16[1,15,320]{2,1,0:T(8,128)(2,1)S(1)}, bf16[1,15,320]{2,1,0:T(8,128)(2,1)}, u32[]{:S(2)}) copy-start(bf16[1,15,320]{2,1,0:T(8,128)(2,1)} %param.29) | copy-start | bytes 28804
  7.2 399.9 %all-gather.6.cloned.1.call-start = ((), (), s32[]{:S(2)}) async-start(), calls=%async_computation.1 | async-start | bytes 3993600 | tf_op jit(solution)/shard_map/all_gather | solution.py:282
  8.7 401.5 %all-gather.8.cloned.1.call-start = ((), (), s32[]{:S(2)}) async-start(), calls=%async_computation.2 | async-start | bytes 3993600 | tf_op jit(solution)/shard_map/all_gather | solution.py:285
  10.2 404.2 %all-gather.10.cloned.1.call-start = ((), (), s32[]{:S(2)}) async-start(), calls=%async_computation.3 | async-start | bytes 9984000 | tf_op jit(solution)/shard_map/all_gather | solution.py:286
  12.0 409.8 %all-gather.12.cloned.1.call-start = ((), (), s32[]{:S(2)}) async-start(), calls=%async_computation.4 | async-start | bytes 9984000 | tf_op jit(solution)/shard_map/all_gather | solution.py:287
  13.7 415.3 %all-gather.14.cloned.1.call-start = ((), (), s32[]{:S(2)}) async-start(), calls=%async_computation.5 | async-start | bytes 5324800 | tf_op jit(solution)/shard_map/all_gather | solution.py:288
  15.1 212.3 %copy-start.124 = (u32[128]{0:T(128)S(1)}, u32[128]{0:T(128)}, u32[]{:S(2)}) copy-start(u32[128]{0:T(128)} %constant.534) | copy-start | bytes 1540
  15.1 213.7 %copy-start.132 = (bf16[1,15]{1,0:T(2,128)(2,1)S(1)}, bf16[1,15]{1,0:T(2,128)(2,1)}, u32[]{:S(2)}) copy-start(bf16[1,15]{1,0:T(2,128)(2,1)} %param.34) | copy-start | bytes 94
  15.1 213.9 %copy-start.133 = (bf16[1,15]{1,0:T(2,128)(2,1)S(1)}, bf16[1,15]{1,0:T(2,128)(2,1)}, u32[]{:S(2)}) copy-start(bf16[1,15]{1,0:T(2,128)(2,1)} %param.35) | copy-start | bytes 94
  15.5 386.9 %copy-start.54 = (bf16[2,64,960]{2,1,0:T(8,128)(2,1)S(1)}, bf16[2,64,960]{2,1,0:T(8,128)(2,1)}, u32[]{:S(2)}) copy-start(bf16[2,64,960]{2,1,0:T(8,128)(2,1)} %param.24) | copy-start | bytes 737284
  23.6 379.6 %all-to-all-start = ((bf16[64,2,2400]{2,1,0:T(2,128)(2,1)}), bf16[64,2,2400]{2,1,0:T(2,128)(2,1)S(1)}, u32[]{:S(2)}, u32[]{:S(2)}) async-start(bf16[64,2,2400]{2,1,0:T(2,128)(2,1)} %reshape.1377), calls=%async_computation | async-start | bytes 1245184 | tf_op jit(solution)/shard_map/all_to_all | solution.py:22
  35.1 1456.8 %all-reduce.7.cloned.1.call-start = ((), (), s32[]{:S(2)}) async-start(), calls=%async_computation.6 | async-start | bytes 78708736
  227.4 489.2 %copy-start.4 = (bf16[1,960,320]{1,2,0:T(8,128)(2,1)}, bf16[1,960,320]{1,2,0:T(8,128)(2,1)S(1)}, u32[]{:S(2)}) copy-start(bf16[1,960,320]{1,2,0:T(8,128)(2,1)S(1)} %copy.455) | copy-start | bytes 1843204
  402.5 314.2 %copy-start.90 = (bf16[960]{0:T(1024)(128)(2,1)}, bf16[960]{0:T(1024)(128)(2,1)S(1)}, u32[]{:S(2)}) copy-start(bf16[960]{0:T(1024)(128)(2,1)S(1)} %get-tuple-element.1183) | copy-start | bytes 5764
  402.5 314.2 %copy-start.94 = (bf16[960]{0:T(1024)(128)(2,1)}, bf16[960]{0:T(1024)(128)(2,1)S(1)}, u32[]{:S(2)}) copy-start(bf16[960]{0:T(1024)(128)(2,1)S(1)} %get-tuple-element.1184) | copy-start | bytes 5764
  407.1 267.9 %copy-start.14 = (bf16[1,960,320]{1,2,0:T(8,128)(2,1)}, bf16[1,960,320]{1,2,0:T(8,128)(2,1)S(1)}, u32[]{:S(2)}) copy-start(bf16[1,960,320]{1,2,0:T(8,128)(2,1)S(1)} %copy.457) | copy-start | bytes 1843204
  468.5 204.9 %collective-permute-start = (bf16[64,960]{1,0:T(8,128)(2,1)}, bf16[64,960]{1,0:T(8,128)(2,1)}, u32[]{:S(2)}, u32[]{:S(2)}) collective-permute-start(bf16[64,960]{1,0:T(8,128)(2,1)} %get-tuple-element.1418), channel_id=1, source_target_pairs={{0,64},{1,65},{2,66},{3,67},{4,68},{5,69},{6,70},{7,71},{8,72},{9,... | collective-permute-start | bytes 368648 | tf_op jit(solution)/shard_map/ppermute | solution.py:30
  706.9 7.5 collective-permute-start.1
  725.9 50.9 %collective-permute-start.2 = (bf16[64,960]{1,0:T(8,128)(2,1)}, bf16[64,960]{1,0:T(8,128)(2,1)}, u32[]{:S(2)}, u32[]{:S(2)}) collective-permute-start(bf16[64,960]{1,0:T(8,128)(2,1)} %get-tuple-element.623), channel_id=1, source_target_pairs={{64,0},{65,1},{66,2},{67,3},{68,4},{69,5},{70,6},{71,7},{72,8},{73... | collective-permute-start | bytes 368648 | tf_op jit(solution)/shard_map/ppermute | solution.py:30
  729.7 47.2 %copy-start.5 = (bf16[1,960,320]{1,2,0:T(8,128)(2,1)S(1)}, bf16[1,960,320]{1,2,0:T(8,128)(2,1)}, u32[]{:S(2)}) copy-start(bf16[1,960,320]{1,2,0:T(8,128)(2,1)} %copy-done.4) | copy-start | bytes 1843204
  729.7 47.2 %copy-start.91 = (bf16[960]{0:T(1024)(128)(2,1)S(1)}, bf16[960]{0:T(1024)(128)(2,1)}, u32[]{:S(2)}) copy-start(bf16[960]{0:T(1024)(128)(2,1)} %copy-done.90) | copy-start | bytes 5764
  729.7 47.2 %copy-start.112 = (s32[2,64]{1,0:T(2,128)S(1)}, s32[2,64]{1,0:T(2,128)}, u32[]{:S(2)}) copy-start(s32[2,64]{1,0:T(2,128)} %param.25) | copy-start | bytes 1540
  734.8 42.1 %copy-start.16 = (bf16[2,64,2560]{2,1,0:T(8,128)(2,1)}, bf16[2,64,2560]{2,1,0:T(8,128)(2,1)S(1)}, u32[]{:S(2)}) copy-start(bf16[2,64,2560]{2,1,0:T(8,128)(2,1)S(1)} %bitcast_dynamic-update-slice_fusion.2) | copy-start | bytes 1966084
  776.9 16.7 %copy-start.10 = (bf16[960,320]{0,1:T(8,128)(2,1)}, bf16[960,320]{0,1:T(8,128)(2,1)S(1)}, u32[]{:S(2)}) copy-start(bf16[960,320]{0,1:T(8,128)(2,1)S(1)} %get-tuple-element.1128) | copy-start | bytes 1843204 | tf_op jit(solution)/shard_map/cond
  796.5 12.3 slice-start.14
  841.5 29.1 %copy-start.17 = (bf16[2,64,2560]{2,1,0:T(8,128)(2,1)S(1)}, bf16[2,64,2560]{2,1,0:T(8,128)(2,1)}, u32[]{:S(2)}) copy-start(bf16[2,64,2560]{2,1,0:T(8,128)(2,1)} %copy-done.16) | copy-start | bytes 1966084
  841.5 39.2 %collective-permute-start.3 = (bf16[64,960]{1,0:T(8,128)(2,1)}, bf16[64,960]{1,0:T(8,128)(2,1)}, u32[]{:S(2)}, u32[]{:S(2)}) collective-permute-start(bf16[64,960]{1,0:T(8,128)(2,1)} %get-tuple-element.624), channel_id=1, source_target_pairs={{64,0},{65,1},{66,2},{67,3},{68,4},{69,5},{70,6},{71,7},{72,8},{73... | collective-permute-start | bytes 368648 | tf_op jit(solution)/shard_map/ppermute | solution.py:30
  844.8 35.9 %copy-start.6 = (bf16[1,960,320]{1,2,0:T(8,128)(2,1)S(1)}, bf16[1,960,320]{1,2,0:T(8,128)(2,1)}, u32[]{:S(2)}) copy-start(bf16[1,960,320]{1,2,0:T(8,128)(2,1)} %copy-done.4) | copy-start | bytes 1843204
  844.8 35.9 %copy-start.92 = (bf16[960]{0:T(1024)(128)(2,1)S(1)}, bf16[960]{0:T(1024)(128)(2,1)}, u32[]{:S(2)}) copy-start(bf16[960]{0:T(1024)(128)(2,1)} %copy-done.90) | copy-start | bytes 5764
  844.8 35.9 %copy-start.113 = (s32[2,64]{1,0:T(2,128)S(1)}, s32[2,64]{1,0:T(2,128)}, u32[]{:S(2)}) copy-start(s32[2,64]{1,0:T(2,128)} %param.25) | copy-start | bytes 1540
  858.6 16.9 %copy-start.52 = (bf16[2,64,320]{2,1,0:T(8,128)(2,1)S(1)}, bf16[2,64,320]{2,1,0:T(8,128)(2,1)}, u32[]{:S(2)}) copy-start(bf16[2,64,320]{2,1,0:T(8,128)(2,1)} %constant_dynamic-update-slice_fusion.1) | copy-start | bytes 245764
  880.9 16.3 %copy-start.12 = (bf16[960,320]{0,1:T(8,128)(2,1)}, bf16[960,320]{0,1:T(8,128)(2,1)S(1)}, u32[]{:S(2)}) copy-start(bf16[960,320]{0,1:T(8,128)(2,1)S(1)} %get-tuple-element.1143) | copy-start | bytes 1843204 | tf_op jit(solution)/shard_map/cond
  900.1 12.3 slice-start.16
  952.2 10.9 copy-start.63
  952.2 11.9 copy-start.53
  958.5 10.0 copy-start.36
  958.7 10.8 copy-start.34
  958.7 10.8 copy-start.56
  987.1 12.0 copy-start.25
  987.1 12.0 copy-start.45
  1006.3 12.0 copy-start.19
  1006.3 12.0 copy-start.43
  1006.3 13.1 copy-start.38
  1006.3 13.1 copy-start.57
  1038.0 12.5 copy-start.26
  1063.3 20.9 %slice-start.18 = ((s8[9830400]{0:T(1024)(128)(4,1)}), s8[1441792]{0:T(1024)(128)(4,1)S(1)}, s32[]{:S(2)}) async-start(s8[9830400]{0:T(1024)(128)(4,1)} %bitcast.935), calls=%async_computation.25 | async-start | bytes 2883584
  1132.4 373.3 %copy-start.69 = (bf16[1,2,64,960]{3,2,1,0:T(8,128)(2,1)}, bf16[1,2,64,960]{3,2,1,0:T(8,128)(2,1)S(1)}, u32[]{:S(2)}) copy-start(bf16[1,2,64,960]{3,2,1,0:T(8,128)(2,1)S(1)} %get-tuple-element.1332) | copy-start | bytes 737284
  (89 other events, 433.5 us)
Sparse Core Ops, SparseCore 0:
  11.4 71.6 all-gather.5
  86.4 66.7 all-gather.7
  156.6 81.3 all-gather.9
  241.3 82.3 all-gather.11
  326.4 69.7 all-gather.13
  1127.0 364.7 all-reduce.6
